TPU v7x, 32 devices: a whole 2x2x4 slice. The times are simulated.
32 devices in a mesh: section: 4 (over y, core), dom: 8 (over z, x).
Axes of the slice: x: 2, y: 2, z: 4, core: 2. Of those that a mesh axis runs over, the one named last changes fastest.
Arguments:
- initial_feat: bfloat16 [2, 2048, 1024], P(None, 'dom'), may hold values from -6 to 6
- layer_weight: bfloat16 [4, 1024, 1024], P('section'), may hold values from -1.35 to 1.35
- tile_column: int32 [8, 2, 2, 4], P('dom'), may hold values from 0 to 1, as said below
- tile_values: bfloat16 [8, 2, 2, 4, 128, 128], P('dom'), may hold values from 0 to 0.05625, as said below
- send_rows: int32 [8, 2, 8, 16], P('dom'), may hold values from 0 to 255
Outputs:
- activations: bfloat16 [4, 2, 2048, 1024], P('section', None, 'dom')
Inputs may be any that keep to these rules, and one draw needn't show every extreme that they name: `tile_column`: each of the two column blocks appears in at least one of the 4 tiles of every partition, node batch and row block. `tile_values`: each row of a tile has a few nonzero weights; the weights of one row over all tiles of its row block sum to about one.
All inputs are finite; a program needn't handle non-finite values.
Results may differ from a plain program's by a relative error of at most 0.006.
Values may be sent and summed in bfloat16 or wider, within the bound.
No kernel may reach another device: no remote copies, remote signals or barrier semaphores. Data moves between devices by JAX's collectives and lax.ppermute only.
A program may use at most 64 MiB of HBM per device.

v0:
```python
import jax
import jax.numpy as jnp
from jax import lax
from jax.sharding import PartitionSpec as P

restart = 0.1
strength = 0.5


def passed_along(x, axis, by):
    devices = lax.axis_size(axis)
    pairs = [(i, i + by) for i in range(devices) if 0 <= i + by < devices]
    return lax.ppermute(x, axis, pairs)


def take_rows(matrix, indices):
    picked = jnp.take(matrix, indices.reshape(-1), axis=0)
    return picked.reshape(indices.shape + (matrix.shape[-1],))


def combine_tiles(current, boundary, tile_weights, tile_block):
    block_count = tile_weights.shape[0]
    side = tile_weights.shape[-1]
    width = current.shape[-1]
    row_blocks = current.reshape(block_count, side, width)
    is_own = (tile_block == 0)[:, :, None, None]
    gathered = jnp.where(is_own, row_blocks[:, None], boundary[None, None])
    summed = jnp.einsum(
        "rtij,rtjf->rif", tile_weights, gathered, preferred_element_type=jnp.float32
    )
    return summed.reshape(block_count * side, width)


def gcn_layer(current, boundary, initial, tile_weights, tile_block, weight_now, beta_mix):
    aggregate = combine_tiles(current, boundary, tile_weights, tile_block)
    mixed_in = ((1.0 - restart) * aggregate + restart * initial.astype(jnp.float32)).astype(
        jnp.bfloat16
    )
    product = jnp.dot(mixed_in, weight_now, preferred_element_type=jnp.float32)
    return jax.nn.relu((1.0 - beta_mix) * mixed_in.astype(jnp.float32) + beta_mix * product).astype(
        jnp.bfloat16
    )


def on_device(initial_feat, layer_weight, tile_column, tile_values, send_rows):
    section_count = lax.axis_size("section")
    section_pos = lax.axis_index("section")
    batch_count = initial_feat.shape[0]
    width = initial_feat.shape[-1]
    side = tile_values.shape[-1]
    layer_pos = (section_pos + 1).astype(jnp.float32)
    beta_mix = jnp.log(strength / layer_pos + 1.0)
    weight_now = layer_weight[0]
    block_all = tile_column[0]
    weights_all = tile_values[0]
    sends_all = send_rows[0]
    tick_count = section_count + batch_count - 1
    stored = jnp.zeros_like(initial_feat)

    def batch_inputs(tick_num):
        batch_num = tick_num - section_pos
        active_now = (batch_num >= 0) & (batch_num < batch_count)
        batch_id = jnp.clip(batch_num, 0, batch_count - 1)
        initial = lax.dynamic_index_in_dim(initial_feat, batch_id, 0, keepdims=False)
        tile_weights = lax.dynamic_index_in_dim(weights_all, batch_id, 0, keepdims=False)
        tile_block = lax.dynamic_index_in_dim(block_all, batch_id, 0, keepdims=False)
        send_now = lax.dynamic_index_in_dim(sends_all, batch_id, 0, keepdims=False)
        return (active_now, batch_id, initial, tile_weights, tile_block, send_now)

    def apply_layer(
        active_now, batch_id, current, boundary, initial, tile_weights, tile_block, stored
    ):

        def compute(operand):
            output = gcn_layer(
                current, boundary, initial, tile_weights, tile_block, weight_now, beta_mix
            )
            return (output, lax.dynamic_update_index_in_dim(stored, output, batch_id, 0))

        def skipped(operand):
            return (jnp.zeros_like(current), stored)

        return lax.cond(active_now, compute, skipped, current)

    def tick_step(tick_num, carry):
        received, stored = carry
        active_now, batch_id, initial, tile_weights, tile_block, send_now = batch_inputs(tick_num)
        current = jnp.where(section_pos == 0, initial, received)
        outgoing = take_rows(current, send_now)
        boundary = lax.all_to_all(outgoing, "dom", split_axis=0, concat_axis=0, tiled=True).reshape(
            side, width
        )
        output, stored = apply_layer(
            active_now, batch_id, current, boundary, initial, tile_weights, tile_block, stored
        )
        received = passed_along(output, "section", 1)
        return (received, stored)

    start_rows = jnp.zeros(initial_feat.shape[1:], jnp.bfloat16)
    finished = lax.fori_loop(0, tick_count, tick_step, (start_rows, stored))
    stored = finished[1]
    return stored[None]


def solution(mesh):
    in_specs = (
        P(None, "dom", None),
        P("section", None, None),
        P("dom", None, None, None),
        P("dom", None, None, None, None, None),
        P("dom", None, None, None),
    )
    out_specs = P("section", None, "dom", None)
    return jax.shard_map(
        on_device, mesh=mesh, in_specs=in_specs, out_specs=out_specs, check_vma=False
    )
```

profile of v0, /device:TPU:1, one launch (start us, length us, event | category | flops | bytes accessed | tf_op | source)
XLA Modules:
  0.0 138.1 jit_solution(13990132352387187109)
XLA Ops:
  0.3 136.9 %while.19 = (s32[]{:T(128)}, bf16[256,1024]{1,0:T(8,128)(2,1)S(1)}, bf16[2,256,1024]{2,1,0:T(8,128)(2,1)S(1)}, s32[]{:T(128)}, pred[]{:T(512)}, /*index=5*/bf16[...) while((s32[]{:T(128)}, bf16[256,1024]{1,0:T(8,128)(2,1)S(1)}, ...), condition=%wide.region_3.4_spmd, body=%wide.region_0.3_spmd.sunk | while | flops 809633920 | bytes 24913448 | solution.py:100
  0.3 0.7 compare_and_fusion.2
  1.1 1.1 broadcast_select_fusion.4
  2.2 0.9 gather_fusion
  3.1 0.8 broadcast_select_fusion.5
  3.9 6.3 %all-to-all-start = ((bf16[8,16,1024]{2,1,0:T(8,128)(2,1)}), bf16[8,16,1024]{2,1,0:T(8,128)(2,1)S(1)}, u32[]{:S(2)}, u32[]{:S(2)}) async-start(bf16[8,16,1024]{2,1,0:T(8,128)(2,1)} %broadcast_select_fusion.5), calls=%async_computation | async-start | bytes 524288 | tf_op jit(solution)/shard_map/while/body/eval_jaxpr/all_to_all | solution.py:90
  10.2 7.4 %all-to-all-done = bf16[8,16,1024]{2,1,0:T(8,128)(2,1)S(1)} async-done(((bf16[8,16,1024]{2,1,0:T(8,128)(2,1)}), bf16[8,16,1024]{2,1,0:T(8,128)(2,1)S(1)}, u32[]{:S(2)}, u32[]{:S(2)}) %all-to-all-start) | async-done | bytes 262176 | tf_op jit(solution)/shard_map/while/body/eval_jaxpr/all_to_all | solution.py:90
  17.7 5.5 %collective-permute-start = (bf16[256,1024]{1,0:T(8,128)(2,1)S(1)}, bf16[256,1024]{1,0:T(8,128)(2,1)S(1)}, u32[]{:S(2)}, u32[]{:S(2)}) collective-permute-start(bf16[256,1024]{1,0:T(8,128)(2,1)S(1)} %get-tuple-element.407), channel_id=1, source_target_pairs={{0,8},{8,16},{16,24},{1,9},{9,17},{17,25},{2,10},{10,18},{18,26},{... | collective-permute-start | bytes 1572872 | tf_op jit(solution)/shard_map/while/body/eval_jaxpr/ppermute | solution.py:13
  23.2 6.1 %collective-permute-done = bf16[256,1024]{1,0:T(8,128)(2,1)S(1)} collective-permute-done((bf16[256,1024]{1,0:T(8,128)(2,1)S(1)}, bf16[256,1024]{1,0:T(8,128)(2,1)S(1)}, u32[]{:S(2)}, u32[]{:S(2)}) %collective-permute-start) | collective-permute-done | bytes 524320 | tf_op jit(solution)/shard_map/while/body/eval_jaxpr/ppermute | solution.py:13
  29.3 0.7 compare_and_fusion.2
  30.1 1.1 broadcast_select_fusion.4
  31.3 0.9 gather_fusion
  32.1 0.8 broadcast_select_fusion.5
  32.9 3.4 %all-to-all-start = ((bf16[8,16,1024]{2,1,0:T(8,128)(2,1)}), bf16[8,16,1024]{2,1,0:T(8,128)(2,1)S(1)}, u32[]{:S(2)}, u32[]{:S(2)}) async-start(bf16[8,16,1024]{2,1,0:T(8,128)(2,1)} %broadcast_select_fusion.5), calls=%async_computation | async-start | bytes 524288 | tf_op jit(solution)/shard_map/while/body/eval_jaxpr/all_to_all | solution.py:90
  36.4 7.0 %all-to-all-done = bf16[8,16,1024]{2,1,0:T(8,128)(2,1)S(1)} async-done(((bf16[8,16,1024]{2,1,0:T(8,128)(2,1)}), bf16[8,16,1024]{2,1,0:T(8,128)(2,1)S(1)}, u32[]{:S(2)}, u32[]{:S(2)}) %all-to-all-start) | async-done | bytes 262176 | tf_op jit(solution)/shard_map/while/body/eval_jaxpr/all_to_all | solution.py:90
  43.4 2.4 %conditional.2 = (bf16[256,1024]{1,0:T(8,128)(2,1)S(1)}, bf16[2,256,1024]{2,1,0:T(8,128)(2,1)S(1)}) conditional(s32[]{:T(128)} %convert_element_type.37, bf16[2,256,1024]{2,1,0:T(8,128)(2,1)S(1)} %get-tuple-element.429, (f32[]{:T(128)}, bf16[2,2,4,128,128]{4,3,2,1,0:T(8,128)(2,1)S(1)}, s32[]{:T(128)}, s32[2,2,4]{2,1,0:T(2,128)S(1)}, ...), branch_computations={%region_1.1_spmd, %region_2.2_spmd} | conditional | flops 809238528 | bytes 16777878 | solution.py:83
  44.1 0.9 copy-done.2
  45.0 0.7 bitcast_dynamic-update-slice_fusion
  45.7 3.5 %collective-permute-start = (bf16[256,1024]{1,0:T(8,128)(2,1)S(1)}, bf16[256,1024]{1,0:T(8,128)(2,1)S(1)}, u32[]{:S(2)}, u32[]{:S(2)}) collective-permute-start(bf16[256,1024]{1,0:T(8,128)(2,1)S(1)} %get-tuple-element.407), channel_id=1, source_target_pairs={{0,8},{8,16},{16,24},{1,9},{9,17},{17,25},{2,10},{10,18},{18,26},{... | collective-permute-start | bytes 1572872 | tf_op jit(solution)/shard_map/while/body/eval_jaxpr/ppermute | solution.py:13
  49.2 6.1 %collective-permute-done = bf16[256,1024]{1,0:T(8,128)(2,1)S(1)} collective-permute-done((bf16[256,1024]{1,0:T(8,128)(2,1)S(1)}, bf16[256,1024]{1,0:T(8,128)(2,1)S(1)}, u32[]{:S(2)}, u32[]{:S(2)}) %collective-permute-start) | collective-permute-done | bytes 524320 | tf_op jit(solution)/shard_map/while/body/eval_jaxpr/ppermute | solution.py:13
  55.3 0.7 compare_and_fusion.2
  56.1 1.1 broadcast_select_fusion.4
  57.3 0.9 gather_fusion
  58.1 0.8 broadcast_select_fusion.5
  58.9 3.4 %all-to-all-start = ((bf16[8,16,1024]{2,1,0:T(8,128)(2,1)}), bf16[8,16,1024]{2,1,0:T(8,128)(2,1)S(1)}, u32[]{:S(2)}, u32[]{:S(2)}) async-start(bf16[8,16,1024]{2,1,0:T(8,128)(2,1)} %broadcast_select_fusion.5), calls=%async_computation | async-start | bytes 524288 | tf_op jit(solution)/shard_map/while/body/eval_jaxpr/all_to_all | solution.py:90
  62.3 7.0 %all-to-all-done = bf16[8,16,1024]{2,1,0:T(8,128)(2,1)S(1)} async-done(((bf16[8,16,1024]{2,1,0:T(8,128)(2,1)}), bf16[8,16,1024]{2,1,0:T(8,128)(2,1)S(1)}, u32[]{:S(2)}, u32[]{:S(2)}) %all-to-all-start) | async-done | bytes 262176 | tf_op jit(solution)/shard_map/while/body/eval_jaxpr/all_to_all | solution.py:90
  69.3 2.4 %conditional.2 = (bf16[256,1024]{1,0:T(8,128)(2,1)S(1)}, bf16[2,256,1024]{2,1,0:T(8,128)(2,1)S(1)}) conditional(s32[]{:T(128)} %convert_element_type.37, bf16[2,256,1024]{2,1,0:T(8,128)(2,1)S(1)} %get-tuple-element.429, (f32[]{:T(128)}, bf16[2,2,4,128,128]{4,3,2,1,0:T(8,128)(2,1)S(1)}, s32[]{:T(128)}, s32[2,2,4]{2,1,0:T(2,128)S(1)}, ...), branch_computations={%region_1.1_spmd, %region_2.2_spmd} | conditional | flops 809238528 | bytes 16777878 | solution.py:83
  70.1 0.9 copy-done.2
  71.0 0.7 bitcast_dynamic-update-slice_fusion
  71.7 5.5 %collective-permute-start = (bf16[256,1024]{1,0:T(8,128)(2,1)S(1)}, bf16[256,1024]{1,0:T(8,128)(2,1)S(1)}, u32[]{:S(2)}, u32[]{:S(2)}) collective-permute-start(bf16[256,1024]{1,0:T(8,128)(2,1)S(1)} %get-tuple-element.407), channel_id=1, source_target_pairs={{0,8},{8,16},{16,24},{1,9},{9,17},{17,25},{2,10},{10,18},{18,26},{... | collective-permute-start | bytes 1572872 | tf_op jit(solution)/shard_map/while/body/eval_jaxpr/ppermute | solution.py:13
  77.3 6.1 %collective-permute-done = bf16[256,1024]{1,0:T(8,128)(2,1)S(1)} collective-permute-done((bf16[256,1024]{1,0:T(8,128)(2,1)S(1)}, bf16[256,1024]{1,0:T(8,128)(2,1)S(1)}, u32[]{:S(2)}, u32[]{:S(2)}) %collective-permute-start) | collective-permute-done | bytes 524320 | tf_op jit(solution)/shard_map/while/body/eval_jaxpr/ppermute | solution.py:13
  83.4 0.7 compare_and_fusion.2
  84.1 1.1 broadcast_select_fusion.4
  85.3 0.9 gather_fusion
  86.2 0.8 broadcast_select_fusion.5
  86.9 3.4 %all-to-all-start = ((bf16[8,16,1024]{2,1,0:T(8,128)(2,1)}), bf16[8,16,1024]{2,1,0:T(8,128)(2,1)S(1)}, u32[]{:S(2)}, u32[]{:S(2)}) async-start(bf16[8,16,1024]{2,1,0:T(8,128)(2,1)} %broadcast_select_fusion.5), calls=%async_computation | async-start | bytes 524288 | tf_op jit(solution)/shard_map/while/body/eval_jaxpr/all_to_all | solution.py:90
  90.4 7.0 %all-to-all-done = bf16[8,16,1024]{2,1,0:T(8,128)(2,1)S(1)} async-done(((bf16[8,16,1024]{2,1,0:T(8,128)(2,1)}), bf16[8,16,1024]{2,1,0:T(8,128)(2,1)S(1)}, u32[]{:S(2)}, u32[]{:S(2)}) %all-to-all-start) | async-done | bytes 262176 | tf_op jit(solution)/shard_map/while/body/eval_jaxpr/all_to_all | solution.py:90
  97.5 7.8 %collective-permute-start = (bf16[256,1024]{1,0:T(8,128)(2,1)S(1)}, bf16[256,1024]{1,0:T(8,128)(2,1)S(1)}, u32[]{:S(2)}, u32[]{:S(2)}) collective-permute-start(bf16[256,1024]{1,0:T(8,128)(2,1)S(1)} %get-tuple-element.407), channel_id=1, source_target_pairs={{0,8},{8,16},{16,24},{1,9},{9,17},{17,25},{2,10},{10,18},{18,26},{... | collective-permute-start | bytes 1572872 | tf_op jit(solution)/shard_map/while/body/eval_jaxpr/ppermute | solution.py:13
  105.3 6.1 %collective-permute-done = bf16[256,1024]{1,0:T(8,128)(2,1)S(1)} collective-permute-done((bf16[256,1024]{1,0:T(8,128)(2,1)S(1)}, bf16[256,1024]{1,0:T(8,128)(2,1)S(1)}, u32[]{:S(2)}, u32[]{:S(2)}) %collective-permute-start) | collective-permute-done | bytes 524320 | tf_op jit(solution)/shard_map/while/body/eval_jaxpr/ppermute | solution.py:13
  111.4 0.7 compare_and_fusion.2
  112.2 1.1 broadcast_select_fusion.4
  113.3 0.9 gather_fusion
  114.2 0.8 broadcast_select_fusion.5
  115.0 3.4 %all-to-all-start = ((bf16[8,16,1024]{2,1,0:T(8,128)(2,1)}), bf16[8,16,1024]{2,1,0:T(8,128)(2,1)S(1)}, u32[]{:S(2)}, u32[]{:S(2)}) async-start(bf16[8,16,1024]{2,1,0:T(8,128)(2,1)} %broadcast_select_fusion.5), calls=%async_computation | async-start | bytes 524288 | tf_op jit(solution)/shard_map/while/body/eval_jaxpr/all_to_all | solution.py:90
  118.4 7.0 %all-to-all-done = bf16[8,16,1024]{2,1,0:T(8,128)(2,1)S(1)} async-done(((bf16[8,16,1024]{2,1,0:T(8,128)(2,1)}), bf16[8,16,1024]{2,1,0:T(8,128)(2,1)S(1)}, u32[]{:S(2)}, u32[]{:S(2)}) %all-to-all-start) | async-done | bytes 262176 | tf_op jit(solution)/shard_map/while/body/eval_jaxpr/all_to_all | solution.py:90
  125.5 5.5 %collective-permute-start = (bf16[256,1024]{1,0:T(8,128)(2,1)S(1)}, bf16[256,1024]{1,0:T(8,128)(2,1)S(1)}, u32[]{:S(2)}, u32[]{:S(2)}) collective-permute-start(bf16[256,1024]{1,0:T(8,128)(2,1)S(1)} %get-tuple-element.407), channel_id=1, source_target_pairs={{0,8},{8,16},{16,24},{1,9},{9,17},{17,25},{2,10},{10,18},{18,26},{... | collective-permute-start | bytes 1572872 | tf_op jit(solution)/shard_map/while/body/eval_jaxpr/ppermute | solution.py:13
  131.0 6.1 %collective-permute-done = bf16[256,1024]{1,0:T(8,128)(2,1)S(1)} collective-permute-done((bf16[256,1024]{1,0:T(8,128)(2,1)S(1)}, bf16[256,1024]{1,0:T(8,128)(2,1)S(1)}, u32[]{:S(2)}, u32[]{:S(2)}) %collective-permute-start) | collective-permute-done | bytes 524320 | tf_op jit(solution)/shard_map/while/body/eval_jaxpr/ppermute | solution.py:13
  137.1 1.0 copy-done
  (52 shorter events, 2.5 us)
Async XLA Ops:
  2.2 15.4 %copy-start.1 = (s32[2,2,4]{2,1,0:T(2,128)S(1)}, s32[2,2,4]{2,1,0:T(2,128)}, u32[]{:S(2)}) copy-start(s32[2,2,4]{2,1,0:T(2,128)} %get-tuple-element.450) | copy-start | bytes 196 | tf_op jit(solution)/shard_map/while
  2.2 15.4 %copy-start.3 = (bf16[2,2,4,128,128]{4,3,2,1,0:T(8,128)(2,1)S(1)}, bf16[2,2,4,128,128]{4,3,2,1,0:T(8,128)(2,1)}, u32[]{:S(2)}) copy-start(bf16[2,2,4,128,128]{4,3,2,1,0:T(8,128)(2,1)} %get-tuple-element.449) | copy-start | bytes 1572868 | tf_op jit(solution)/shard_map/while
  3.9 13.8 %all-to-all-start = ((bf16[8,16,1024]{2,1,0:T(8,128)(2,1)}), bf16[8,16,1024]{2,1,0:T(8,128)(2,1)S(1)}, u32[]{:S(2)}, u32[]{:S(2)}) async-start(bf16[8,16,1024]{2,1,0:T(8,128)(2,1)} %broadcast_select_fusion.5), calls=%async_computation | async-start | bytes 524288 | tf_op jit(solution)/shard_map/while/body/eval_jaxpr/all_to_all | solution.py:90
  17.7 11.6 %collective-permute-start = (bf16[256,1024]{1,0:T(8,128)(2,1)S(1)}, bf16[256,1024]{1,0:T(8,128)(2,1)S(1)}, u32[]{:S(2)}, u32[]{:S(2)}) collective-permute-start(bf16[256,1024]{1,0:T(8,128)(2,1)S(1)} %get-tuple-element.407), channel_id=1, source_target_pairs={{0,8},{8,16},{16,24},{1,9},{9,17},{17,25},{2,10},{10,18},{18,26},{... | collective-permute-start | bytes 1572872 | tf_op jit(solution)/shard_map/while/body/eval_jaxpr/ppermute | solution.py:13
  31.2 12.1 %copy-start.1 = (s32[2,2,4]{2,1,0:T(2,128)S(1)}, s32[2,2,4]{2,1,0:T(2,128)}, u32[]{:S(2)}) copy-start(s32[2,2,4]{2,1,0:T(2,128)} %get-tuple-element.450) | copy-start | bytes 196 | tf_op jit(solution)/shard_map/while
  31.3 12.1 %copy-start.3 = (bf16[2,2,4,128,128]{4,3,2,1,0:T(8,128)(2,1)S(1)}, bf16[2,2,4,128,128]{4,3,2,1,0:T(8,128)(2,1)}, u32[]{:S(2)}) copy-start(bf16[2,2,4,128,128]{4,3,2,1,0:T(8,128)(2,1)} %get-tuple-element.449) | copy-start | bytes 1572868 | tf_op jit(solution)/shard_map/while
  32.9 10.4 %all-to-all-start = ((bf16[8,16,1024]{2,1,0:T(8,128)(2,1)}), bf16[8,16,1024]{2,1,0:T(8,128)(2,1)S(1)}, u32[]{:S(2)}, u32[]{:S(2)}) async-start(bf16[8,16,1024]{2,1,0:T(8,128)(2,1)} %broadcast_select_fusion.5), calls=%async_computation | async-start | bytes 524288 | tf_op jit(solution)/shard_map/while/body/eval_jaxpr/all_to_all | solution.py:90
  43.4 1.6 %copy-start.2 = (bf16[1024,1024]{1,0:T(8,128)(2,1)S(1)}, bf16[1024,1024]{1,0:T(8,128)(2,1)}, u32[]{:S(2)}) copy-start(bf16[1024,1024]{1,0:T(8,128)(2,1)} %get-tuple-element.284) | copy-start | bytes 6291460 | tf_op jit(solution)/shard_map/while/body/eval_jaxpr/cond
  45.7 9.6 %collective-permute-start = (bf16[256,1024]{1,0:T(8,128)(2,1)S(1)}, bf16[256,1024]{1,0:T(8,128)(2,1)S(1)}, u32[]{:S(2)}, u32[]{:S(2)}) collective-permute-start(bf16[256,1024]{1,0:T(8,128)(2,1)S(1)} %get-tuple-element.407), channel_id=1, source_target_pairs={{0,8},{8,16},{16,24},{1,9},{9,17},{17,25},{2,10},{10,18},{18,26},{... | collective-permute-start | bytes 1572872 | tf_op jit(solution)/shard_map/while/body/eval_jaxpr/ppermute | solution.py:13
  57.2 12.1 %copy-start.1 = (s32[2,2,4]{2,1,0:T(2,128)S(1)}, s32[2,2,4]{2,1,0:T(2,128)}, u32[]{:S(2)}) copy-start(s32[2,2,4]{2,1,0:T(2,128)} %get-tuple-element.450) | copy-start | bytes 196 | tf_op jit(solution)/shard_map/while
  57.2 12.1 %copy-start.3 = (bf16[2,2,4,128,128]{4,3,2,1,0:T(8,128)(2,1)S(1)}, bf16[2,2,4,128,128]{4,3,2,1,0:T(8,128)(2,1)}, u32[]{:S(2)}) copy-start(bf16[2,2,4,128,128]{4,3,2,1,0:T(8,128)(2,1)} %get-tuple-element.449) | copy-start | bytes 1572868 | tf_op jit(solution)/shard_map/while
  58.9 10.4 %all-to-all-start = ((bf16[8,16,1024]{2,1,0:T(8,128)(2,1)}), bf16[8,16,1024]{2,1,0:T(8,128)(2,1)S(1)}, u32[]{:S(2)}, u32[]{:S(2)}) async-start(bf16[8,16,1024]{2,1,0:T(8,128)(2,1)} %broadcast_select_fusion.5), calls=%async_computation | async-start | bytes 524288 | tf_op jit(solution)/shard_map/while/body/eval_jaxpr/all_to_all | solution.py:90
  69.4 1.6 %copy-start.2 = (bf16[1024,1024]{1,0:T(8,128)(2,1)S(1)}, bf16[1024,1024]{1,0:T(8,128)(2,1)}, u32[]{:S(2)}) copy-start(bf16[1024,1024]{1,0:T(8,128)(2,1)} %get-tuple-element.284) | copy-start | bytes 6291460 | tf_op jit(solution)/shard_map/while/body/eval_jaxpr/cond
  71.7 11.6 %collective-permute-start = (bf16[256,1024]{1,0:T(8,128)(2,1)S(1)}, bf16[256,1024]{1,0:T(8,128)(2,1)S(1)}, u32[]{:S(2)}, u32[]{:S(2)}) collective-permute-start(bf16[256,1024]{1,0:T(8,128)(2,1)S(1)} %get-tuple-element.407), channel_id=1, source_target_pairs={{0,8},{8,16},{16,24},{1,9},{9,17},{17,25},{2,10},{10,18},{18,26},{... | collective-permute-start | bytes 1572872 | tf_op jit(solution)/shard_map/while/body/eval_jaxpr/ppermute | solution.py:13
  85.3 12.1 %copy-start.1 = (s32[2,2,4]{2,1,0:T(2,128)S(1)}, s32[2,2,4]{2,1,0:T(2,128)}, u32[]{:S(2)}) copy-start(s32[2,2,4]{2,1,0:T(2,128)} %get-tuple-element.450) | copy-start | bytes 196 | tf_op jit(solution)/shard_map/while
  85.3 12.1 %copy-start.3 = (bf16[2,2,4,128,128]{4,3,2,1,0:T(8,128)(2,1)S(1)}, bf16[2,2,4,128,128]{4,3,2,1,0:T(8,128)(2,1)}, u32[]{:S(2)}) copy-start(bf16[2,2,4,128,128]{4,3,2,1,0:T(8,128)(2,1)} %get-tuple-element.449) | copy-start | bytes 1572868 | tf_op jit(solution)/shard_map/while
  86.9 10.4 %all-to-all-start = ((bf16[8,16,1024]{2,1,0:T(8,128)(2,1)}), bf16[8,16,1024]{2,1,0:T(8,128)(2,1)S(1)}, u32[]{:S(2)}, u32[]{:S(2)}) async-start(bf16[8,16,1024]{2,1,0:T(8,128)(2,1)} %broadcast_select_fusion.5), calls=%async_computation | async-start | bytes 524288 | tf_op jit(solution)/shard_map/while/body/eval_jaxpr/all_to_all | solution.py:90
  97.5 13.9 %collective-permute-start = (bf16[256,1024]{1,0:T(8,128)(2,1)S(1)}, bf16[256,1024]{1,0:T(8,128)(2,1)S(1)}, u32[]{:S(2)}, u32[]{:S(2)}) collective-permute-start(bf16[256,1024]{1,0:T(8,128)(2,1)S(1)} %get-tuple-element.407), channel_id=1, source_target_pairs={{0,8},{8,16},{16,24},{1,9},{9,17},{17,25},{2,10},{10,18},{18,26},{... | collective-permute-start | bytes 1572872 | tf_op jit(solution)/shard_map/while/body/eval_jaxpr/ppermute | solution.py:13
  113.3 12.1 %copy-start.1 = (s32[2,2,4]{2,1,0:T(2,128)S(1)}, s32[2,2,4]{2,1,0:T(2,128)}, u32[]{:S(2)}) copy-start(s32[2,2,4]{2,1,0:T(2,128)} %get-tuple-element.450) | copy-start | bytes 196 | tf_op jit(solution)/shard_map/while
  113.3 12.1 %copy-start.3 = (bf16[2,2,4,128,128]{4,3,2,1,0:T(8,128)(2,1)S(1)}, bf16[2,2,4,128,128]{4,3,2,1,0:T(8,128)(2,1)}, u32[]{:S(2)}) copy-start(bf16[2,2,4,128,128]{4,3,2,1,0:T(8,128)(2,1)} %get-tuple-element.449) | copy-start | bytes 1572868 | tf_op jit(solution)/shard_map/while
  115.0 10.4 %all-to-all-start = ((bf16[8,16,1024]{2,1,0:T(8,128)(2,1)}), bf16[8,16,1024]{2,1,0:T(8,128)(2,1)S(1)}, u32[]{:S(2)}, u32[]{:S(2)}) async-start(bf16[8,16,1024]{2,1,0:T(8,128)(2,1)} %broadcast_select_fusion.5), calls=%async_computation | async-start | bytes 524288 | tf_op jit(solution)/shard_map/while/body/eval_jaxpr/all_to_all | solution.py:90
  125.5 11.7 %collective-permute-start = (bf16[256,1024]{1,0:T(8,128)(2,1)S(1)}, bf16[256,1024]{1,0:T(8,128)(2,1)S(1)}, u32[]{:S(2)}, u32[]{:S(2)}) collective-permute-start(bf16[256,1024]{1,0:T(8,128)(2,1)S(1)} %get-tuple-element.407), channel_id=1, source_target_pairs={{0,8},{8,16},{16,24},{1,9},{9,17},{17,25},{2,10},{10,18},{18,26},{... | collective-permute-start | bytes 1572872 | tf_op jit(solution)/shard_map/while/body/eval_jaxpr/ppermute | solution.py:13
  137.1 1.0 copy-start
where the time goes:
time: 139 us; the launch traced here: 138 us
  waiting for transfers between devices  65.9 us (47%)
  starting transfers between devices  47.9 us (34%)
  other arithmetic  13.4 us (10%)
  local copies, waits for them, and re-layouts  7.81 us (6%)
  matrix products  2.58 us (2%)
    all_to_all x5, waiting for transfers between devices, tick_step(): lax.all_to_all(outgoing, 'dom', split_axis=0, concat_axis=0, tiled=True)  35.4 us
    ppermute x5, waiting for transfers between devices, passed_along(): return lax.ppermute(x, axis, pairs)  30.5 us
    ppermute x5, starting transfers between devices, passed_along(): return lax.ppermute(x, axis, pairs)  27.9 us
    all_to_all x5, starting transfers between devices, tick_step(): lax.all_to_all(outgoing, 'dom', split_axis=0, concat_axis=0, tiled=True)  20 us
    select_n x5, other arithmetic, tick_step(): current = jnp.where(section_pos == 0, initial, received)  5.59 us
    gather x5, local copies, waits for them, and re-layouts, take_rows(): picked = jnp.take(matrix, indices.reshape(-1), axis=0)  4.31 us
    select_n x10, other arithmetic, take_rows(): picked = jnp.take(matrix, indices.reshape(-1), axis=0)  4.02 us
    and x5, other arithmetic, take_rows(): picked = jnp.take(matrix, indices.reshape(-1), axis=0)  3.47 us
  transfers between devices with their start and end apart: 10, of which 10 were waited for; matrix products, arithmetic and copies ran while one was open for 0% of the time, Pallas kernels for 0%

commit v1 on v0

--- a/solution.py
+++ b/solution.py
@@ -5,6 +5,18 @@
 
 restart = 0.1
 strength = 0.5
+
+
+def sent_to_each(x, axis, split, join):
+    ways, here = (lax.axis_size(axis), lax.axis_index(axis))
+    width = x.shape[split] // ways
+    turned = jnp.roll(x, -here * width, axis=split)
+    got = [lax.slice_in_dim(turned, 0, width, axis=split)]
+    for far in range(1, ways):
+        sent = lax.slice_in_dim(turned, far * width, (far + 1) * width, axis=split)
+        got.append(lax.ppermute(sent, axis, [(d, (d + far) % ways) for d in range(ways)]))
+    line = jnp.concatenate(got[::-1], axis=join)
+    return jnp.roll(line, (here + 1) * got[0].shape[join], axis=join)
 
 
 def passed_along(x, axis, by):
@@ -87,9 +99,7 @@
         active_now, batch_id, initial, tile_weights, tile_block, send_now = batch_inputs(tick_num)
         current = jnp.where(section_pos == 0, initial, received)
         outgoing = take_rows(current, send_now)
-        boundary = lax.all_to_all(outgoing, "dom", split_axis=0, concat_axis=0, tiled=True).reshape(
-            side, width
-        )
+        boundary = sent_to_each(outgoing, "dom", 0, 0).reshape(side, width)
         output, stored = apply_layer(
             active_now, batch_id, current, boundary, initial, tile_weights, tile_block, stored
         )

time: 139 us -> 147 us (1.058)
  starting transfers between devices: 47.9 us -> 71.9 us
  waiting for transfers between devices: 65.9 us -> 52 us
  other arithmetic: 13.4 us -> 10.7 us
  matrix products: 2.58 us -> 4.76 us
  local copies, waits for them, and re-layouts: 7.81 us -> 6.32 us
    ppermute x0 -> x35, starting transfers between devices: none -> 37.1 us  [sent_to_each(): lax.ppermute(sent, axis, [(d, (d + far) % ways) for d in range(ways)])]
    all_to_all x5 -> x0, waiting for transfers between devices: 35.4 us -> none  [tick_step(): lax.all_to_all(outgoing, 'dom', split_axis=0, concat_axis=0, tiled=True)]
    ppermute x0 -> x35, waiting for transfers between devices: none -> 21.5 us  [sent_to_each(): lax.ppermute(sent, axis, [(d, (d + far) % ways) for d in range(ways)])]
    all_to_all x5 -> x0, starting transfers between devices: 20 us -> none  [tick_step(): lax.all_to_all(outgoing, 'dom', split_axis=0, concat_axis=0, tiled=True)]
    ppermute x5, starting transfers between devices: 27.9 us -> 34.8 us  [passed_along(): return lax.ppermute(x, axis, pairs)]
    select_n x10, other arithmetic: 4.02 us -> 0.49 us  [take_rows(): picked = jnp.take(matrix, indices.reshape(-1), axis=0)]
    dot_general x2, matrix products: 1.09 us -> 3.26 us  [combine_tiles(): jnp.einsum('rtij,rtjf->rif', tile_weights, gathered, preferred_element_ty...]
    cond x4, local copies, waits for them, and re-layouts: 1.75 us -> 0.01 us
  transfers between devices with their start and end apart: 10 -> 40, of which waited for: 10 -> 21; matrix products, arithmetic and copies ran while one was open for 0% -> 0% of each run, Pallas kernels for 0% -> 0%
where the time goes in v1:
time: 147 us
  starting transfers between devices  71.9 us (49%)
  waiting for transfers between devices  52 us (35%)
  other arithmetic  10.7 us (7%)
  local copies, waits for them, and re-layouts  6.32 us (4%)
  matrix products  4.76 us (3%)
    ppermute x35, starting transfers between devices, sent_to_each(): lax.ppermute(sent, axis, [(d, (d + far) % ways) for d in range(ways)])  37.1 us
    ppermute x5, starting transfers between devices, passed_along(): return lax.ppermute(x, axis, pairs)  34.8 us
    ppermute x5, waiting for transfers between devices, passed_along(): return lax.ppermute(x, axis, pairs)  30.5 us
    ppermute x35, waiting for transfers between devices, sent_to_each(): lax.ppermute(sent, axis, [(d, (d + far) % ways) for d in range(ways)])  21.5 us
    select_n x5, other arithmetic, tick_step(): current = jnp.where(section_pos == 0, initial, received)  5.59 us
    gather x5, local copies, waits for them, and re-layouts, take_rows(): picked = jnp.take(matrix, indices.reshape(-1), axis=0)  4.31 us
    and x5, other arithmetic, take_rows(): picked = jnp.take(matrix, indices.reshape(-1), axis=0)  3.47 us
    dot_general x2, matrix products, combine_tiles(): jnp.einsum('rtij,rtjf->rif', tile_weights, gathered, preferred_element_ty...  3.26 us
  transfers between devices with their start and end apart: 40, of which 21 were waited for; matrix products, arithmetic and copies ran while one was open for 0% of the time, Pallas kernels for 0%

profile of v1, /device:TPU:1, one launch (start us, length us, event | category | flops | bytes accessed | tf_op | source)
XLA Modules:
  0.0 146.5 jit_solution(2590009291000908917)
XLA Ops:
  0.3 145.3 %while.19 = (s32[]{:T(128)}, bf16[256,1024]{1,0:T(8,128)(2,1)S(1)}, bf16[2,256,1024]{2,1,0:T(8,128)(2,1)S(1)}, s32[]{:T(128)}, pred[]{:T(512)}, /*index=5*/bf16[...) while((s32[]{:T(128)}, bf16[256,1024]{1,0:T(8,128)(2,1)S(1)}, ...), condition=%wide.region_3.5_spmd, body=%wide.region_0.4_spmd.sunk | while | flops 810027200 | bytes 25766064 | solution.py:110
  1.1 1.1 broadcast_select_fusion.4
  3.4 5.1 %collective-permute-start = (bf16[1,16,1024]{2,1,0:T(8,128)(2,1)S(1)}, bf16[1,16,1024]{2,1,0:T(8,128)(2,1)S(1)}, u32[]{:S(2)}, u32[]{:S(2)}) collective-permute-start(bf16[1,16,1024]{2,1,0:T(8,128)(2,1)S(1)} %get-tuple-element.459), channel_id=1, source_target_pairs={{0,7},{1,0},{2,1},{3,2},{4,3},{5,4},{6,5},{7,6},{8,15},{9,8},{10,9... | collective-permute-start | bytes 98312 | tf_op jit(solution)/shard_map/while/body/eval_jaxpr/ppermute | solution.py:17
  8.7 2.4 %collective-permute-start.3 = (bf16[1,16,1024]{2,1,0:T(8,128)(2,1)S(1)}, bf16[1,16,1024]{2,1,0:T(8,128)(2,1)S(1)}, u32[]{:S(2)}, u32[]{:S(2)}) collective-permute-start(bf16[1,16,1024]{2,1,0:T(8,128)(2,1)S(1)} %get-tuple-element.462), channel_id=1, source_target_pairs={{0,4},{1,5},{2,6},{3,7},{4,0},{5,1},{6,2},{7,3},{8,12},{9,13},{10,... | collective-permute-start | bytes 98312 | tf_op jit(solution)/shard_map/while/body/eval_jaxpr/ppermute | solution.py:17
  11.1 1.3 collective-permute-start.5
  12.4 1.1 collective-permute-start.6
  13.6 2.3 %collective-permute-done.4 = bf16[1,16,1024]{2,1,0:T(8,128)(2,1)S(1)} collective-permute-done((bf16[1,16,1024]{2,1,0:T(8,128)(2,1)S(1)}, bf16[1,16,1024]{2,1,0:T(8,128)(2,1)S(1)}, u32[]{:S(2)}, u32[]{:S(2)}) %collective-permute-start.4) | collective-permute-done | bytes 32800 | tf_op jit(solution)/shard_map/while/body/eval_jaxpr/ppermute | solution.py:17
  15.8 1.1 collective-permute-done.5
  18.0 6.5 %collective-permute-start.7 = (bf16[256,1024]{1,0:T(8,128)(2,1)S(1)}, bf16[256,1024]{1,0:T(8,128)(2,1)S(1)}, u32[]{:S(2)}, u32[]{:S(2)}) collective-permute-start(bf16[256,1024]{1,0:T(8,128)(2,1)S(1)} %get-tuple-element.467), channel_id=1, source_target_pairs={{0,8},{8,16},{16,24},{1,9},{9,17},{17,25},{2,10},{10,18},{18,26},{... | collective-permute-start | bytes 1572872 | tf_op jit(solution)/shard_map/while/body/eval_jaxpr/ppermute | solution.py:25
  24.5 6.1 %collective-permute-done.7 = bf16[256,1024]{1,0:T(8,128)(2,1)S(1)} collective-permute-done((bf16[256,1024]{1,0:T(8,128)(2,1)S(1)}, bf16[256,1024]{1,0:T(8,128)(2,1)S(1)}, u32[]{:S(2)}, u32[]{:S(2)}) %collective-permute-start.7) | collective-permute-done | bytes 524320 | tf_op jit(solution)/shard_map/while/body/eval_jaxpr/ppermute | solution.py:25
  31.4 1.1 broadcast_select_fusion.4
  33.7 1.1 collective-permute-start.1
  34.9 1.5 collective-permute-start.2
  36.3 1.9 %collective-permute-start.3 = (bf16[1,16,1024]{2,1,0:T(8,128)(2,1)S(1)}, bf16[1,16,1024]{2,1,0:T(8,128)(2,1)S(1)}, u32[]{:S(2)}, u32[]{:S(2)}) collective-permute-start(bf16[1,16,1024]{2,1,0:T(8,128)(2,1)S(1)} %get-tuple-element.462), channel_id=1, source_target_pairs={{0,4},{1,5},{2,6},{3,7},{4,0},{5,1},{6,2},{7,3},{8,12},{9,13},{10,... | collective-permute-start | bytes 98312 | tf_op jit(solution)/shard_map/while/body/eval_jaxpr/ppermute | solution.py:17
  38.2 1.7 %collective-permute-start.5 = (bf16[1,16,1024]{2,1,0:T(8,128)(2,1)S(1)}, bf16[1,16,1024]{2,1,0:T(8,128)(2,1)S(1)}, u32[]{:S(2)}, u32[]{:S(2)}) collective-permute-start(bf16[1,16,1024]{2,1,0:T(8,128)(2,1)S(1)} %get-tuple-element.464), channel_id=1, source_target_pairs={{0,2},{1,3},{2,4},{3,5},{4,6},{5,7},{6,0},{7,1},{8,10},{9,11},{10,... | collective-permute-start | bytes 98312 | tf_op jit(solution)/shard_map/while/body/eval_jaxpr/ppermute | solution.py:17
  40.0 1.4 collective-permute-start.6
  41.5 1.2 collective-permute-done.4
  42.8 2.6 %collective-permute-done.6 = bf16[1,16,1024]{2,1,0:T(8,128)(2,1)S(1)} collective-permute-done((bf16[1,16,1024]{2,1,0:T(8,128)(2,1)S(1)}, bf16[1,16,1024]{2,1,0:T(8,128)(2,1)S(1)}, u32[]{:S(2)}, u32[]{:S(2)}) %collective-permute-start.6) | collective-permute-done | bytes 32800 | tf_op jit(solution)/shard_map/while/body/eval_jaxpr/ppermute | solution.py:17
  45.5 2.7 %conditional.2 = (bf16[256,1024]{1,0:T(8,128)(2,1)S(1)}, bf16[2,256,1024]{2,1,0:T(8,128)(2,1)S(1)}) conditional(s32[]{:T(128)} %convert_element_type.41, bf16[2,256,1024]{2,1,0:T(8,128)(2,1)S(1)} %get-tuple-element.493, (f32[]{:T(128)}, bf16[2,2,4,128,128]{4,3,2,1,0:T(8,128)(2,1)}, s32[]{:T(128)}, s32[2,2,4]{2,1,0:T(2,128)S(1)}, ...), branch_computations={%region_1.2_spmd, %region_2.3_spmd.clone} | conditional | flops 809238528 | bytes 17302208 | solution.py:95
  45.6 1.6 %fusion.8 = f32[2,128,1024]{2,1,0:T(8,128)S(1)} fusion(pred[2,4]{1,0:T(4,128)(4,1)S(1)} %compare_bitcast_fusion, bf16[128,1024]{1,0:T(8,128)(2,1)S(1)} %bitcast.50, bf16[2,128,1024]{2,1,0:T(8,128)(2,1)S(1)} %bitcast.48, bf16[2,2,4,128,128]{4,3,2,1,0:T(8,128)(2,1)} %get-tuple-element.314, s32[]{:T(128)} %get-tuple-element.315), kind=kOutput, calls=%fused_computation.8 | convolution fusion | flops 269746176 | bytes 2097672 | tf_op jit(solution)/shard_map/while/body/eval_jaxpr/cond/branch_1_fun/rtij,rtjf->rif/dot_general | solution.py:40
  48.1 4.4 %collective-permute-start.7 = (bf16[256,1024]{1,0:T(8,128)(2,1)S(1)}, bf16[256,1024]{1,0:T(8,128)(2,1)S(1)}, u32[]{:S(2)}, u32[]{:S(2)}) collective-permute-start(bf16[256,1024]{1,0:T(8,128)(2,1)S(1)} %get-tuple-element.467), channel_id=1, source_target_pairs={{0,8},{8,16},{16,24},{1,9},{9,17},{17,25},{2,10},{10,18},{18,26},{... | collective-permute-start | bytes 1572872 | tf_op jit(solution)/shard_map/while/body/eval_jaxpr/ppermute | solution.py:25
  52.5 6.1 %collective-permute-done.7 = bf16[256,1024]{1,0:T(8,128)(2,1)S(1)} collective-permute-done((bf16[256,1024]{1,0:T(8,128)(2,1)S(1)}, bf16[256,1024]{1,0:T(8,128)(2,1)S(1)}, u32[]{:S(2)}, u32[]{:S(2)}) %collective-permute-start.7) | collective-permute-done | bytes 524320 | tf_op jit(solution)/shard_map/while/body/eval_jaxpr/ppermute | solution.py:25
  59.4 1.1 broadcast_select_fusion.4
  62.8 2.4 %collective-permute-start.3 = (bf16[1,16,1024]{2,1,0:T(8,128)(2,1)S(1)}, bf16[1,16,1024]{2,1,0:T(8,128)(2,1)S(1)}, u32[]{:S(2)}, u32[]{:S(2)}) collective-permute-start(bf16[1,16,1024]{2,1,0:T(8,128)(2,1)S(1)} %get-tuple-element.462), channel_id=1, source_target_pairs={{0,4},{1,5},{2,6},{3,7},{4,0},{5,1},{6,2},{7,3},{8,12},{9,13},{10,... | collective-permute-start | bytes 98312 | tf_op jit(solution)/shard_map/while/body/eval_jaxpr/ppermute | solution.py:17
  65.4 1.6 %collective-permute-start.5 = (bf16[1,16,1024]{2,1,0:T(8,128)(2,1)S(1)}, bf16[1,16,1024]{2,1,0:T(8,128)(2,1)S(1)}, u32[]{:S(2)}, u32[]{:S(2)}) collective-permute-start(bf16[1,16,1024]{2,1,0:T(8,128)(2,1)S(1)} %get-tuple-element.464), channel_id=1, source_target_pairs={{0,2},{1,3},{2,4},{3,5},{4,6},{5,7},{6,0},{7,1},{8,10},{9,11},{10,... | collective-permute-start | bytes 98312 | tf_op jit(solution)/shard_map/while/body/eval_jaxpr/ppermute | solution.py:17
  68.0 1.9 %collective-permute-done.4 = bf16[1,16,1024]{2,1,0:T(8,128)(2,1)S(1)} collective-permute-done((bf16[1,16,1024]{2,1,0:T(8,128)(2,1)S(1)}, bf16[1,16,1024]{2,1,0:T(8,128)(2,1)S(1)}, u32[]{:S(2)}, u32[]{:S(2)}) %collective-permute-start.4) | collective-permute-done | bytes 32800 | tf_op jit(solution)/shard_map/while/body/eval_jaxpr/ppermute | solution.py:17
  70.4 2.1 %collective-permute-done.6 = bf16[1,16,1024]{2,1,0:T(8,128)(2,1)S(1)} collective-permute-done((bf16[1,16,1024]{2,1,0:T(8,128)(2,1)S(1)}, bf16[1,16,1024]{2,1,0:T(8,128)(2,1)S(1)}, u32[]{:S(2)}, u32[]{:S(2)}) %collective-permute-start.6) | collective-permute-done | bytes 32800 | tf_op jit(solution)/shard_map/while/body/eval_jaxpr/ppermute | solution.py:17
  72.5 2.7 %conditional.2 = (bf16[256,1024]{1,0:T(8,128)(2,1)S(1)}, bf16[2,256,1024]{2,1,0:T(8,128)(2,1)S(1)}) conditional(s32[]{:T(128)} %convert_element_type.41, bf16[2,256,1024]{2,1,0:T(8,128)(2,1)S(1)} %get-tuple-element.493, (f32[]{:T(128)}, bf16[2,2,4,128,128]{4,3,2,1,0:T(8,128)(2,1)}, s32[]{:T(128)}, s32[2,2,4]{2,1,0:T(2,128)S(1)}, ...), branch_computations={%region_1.2_spmd, %region_2.3_spmd.clone} | conditional | flops 809238528 | bytes 17302208 | solution.py:95
  72.6 1.6 %fusion.8 = f32[2,128,1024]{2,1,0:T(8,128)S(1)} fusion(pred[2,4]{1,0:T(4,128)(4,1)S(1)} %compare_bitcast_fusion, bf16[128,1024]{1,0:T(8,128)(2,1)S(1)} %bitcast.50, bf16[2,128,1024]{2,1,0:T(8,128)(2,1)S(1)} %bitcast.48, bf16[2,2,4,128,128]{4,3,2,1,0:T(8,128)(2,1)} %get-tuple-element.314, s32[]{:T(128)} %get-tuple-element.315), kind=kOutput, calls=%fused_computation.8 | convolution fusion | flops 269746176 | bytes 2097672 | tf_op jit(solution)/shard_map/while/body/eval_jaxpr/cond/branch_1_fun/rtij,rtjf->rif/dot_general | solution.py:40
  75.2 7.2 %collective-permute-start.7 = (bf16[256,1024]{1,0:T(8,128)(2,1)S(1)}, bf16[256,1024]{1,0:T(8,128)(2,1)S(1)}, u32[]{:S(2)}, u32[]{:S(2)}) collective-permute-start(bf16[256,1024]{1,0:T(8,128)(2,1)S(1)} %get-tuple-element.467), channel_id=1, source_target_pairs={{0,8},{8,16},{16,24},{1,9},{9,17},{17,25},{2,10},{10,18},{18,26},{... | collective-permute-start | bytes 1572872 | tf_op jit(solution)/shard_map/while/body/eval_jaxpr/ppermute | solution.py:25
  82.4 6.1 %collective-permute-done.7 = bf16[256,1024]{1,0:T(8,128)(2,1)S(1)} collective-permute-done((bf16[256,1024]{1,0:T(8,128)(2,1)S(1)}, bf16[256,1024]{1,0:T(8,128)(2,1)S(1)}, u32[]{:S(2)}, u32[]{:S(2)}) %collective-permute-start.7) | collective-permute-done | bytes 524320 | tf_op jit(solution)/shard_map/while/body/eval_jaxpr/ppermute | solution.py:25
  89.3 1.1 broadcast_select_fusion.4
  91.6 1.4 collective-permute-start.1
  93.1 2.1 %collective-permute-start.3 = (bf16[1,16,1024]{2,1,0:T(8,128)(2,1)S(1)}, bf16[1,16,1024]{2,1,0:T(8,128)(2,1)S(1)}, u32[]{:S(2)}, u32[]{:S(2)}) collective-permute-start(bf16[1,16,1024]{2,1,0:T(8,128)(2,1)S(1)} %get-tuple-element.462), channel_id=1, source_target_pairs={{0,4},{1,5},{2,6},{3,7},{4,0},{5,1},{6,2},{7,3},{8,12},{9,13},{10,... | collective-permute-start | bytes 98312 | tf_op jit(solution)/shard_map/while/body/eval_jaxpr/ppermute | solution.py:17
  95.5 1.2 collective-permute-start.5
  96.7 1.4 collective-permute-start.6
  98.1 1.7 %collective-permute-done.4 = bf16[1,16,1024]{2,1,0:T(8,128)(2,1)S(1)} collective-permute-done((bf16[1,16,1024]{2,1,0:T(8,128)(2,1)S(1)}, bf16[1,16,1024]{2,1,0:T(8,128)(2,1)S(1)}, u32[]{:S(2)}, u32[]{:S(2)}) %collective-permute-start.4) | collective-permute-done | bytes 32800 | tf_op jit(solution)/shard_map/while/body/eval_jaxpr/ppermute | solution.py:17
  100.2 2.0 %collective-permute-done.6 = bf16[1,16,1024]{2,1,0:T(8,128)(2,1)S(1)} collective-permute-done((bf16[1,16,1024]{2,1,0:T(8,128)(2,1)S(1)}, bf16[1,16,1024]{2,1,0:T(8,128)(2,1)S(1)}, u32[]{:S(2)}, u32[]{:S(2)}) %collective-permute-start.6) | collective-permute-done | bytes 32800 | tf_op jit(solution)/shard_map/while/body/eval_jaxpr/ppermute | solution.py:17
  102.3 9.5 %collective-permute-start.7 = (bf16[256,1024]{1,0:T(8,128)(2,1)S(1)}, bf16[256,1024]{1,0:T(8,128)(2,1)S(1)}, u32[]{:S(2)}, u32[]{:S(2)}) collective-permute-start(bf16[256,1024]{1,0:T(8,128)(2,1)S(1)} %get-tuple-element.467), channel_id=1, source_target_pairs={{0,8},{8,16},{16,24},{1,9},{9,17},{17,25},{2,10},{10,18},{18,26},{... | collective-permute-start | bytes 1572872 | tf_op jit(solution)/shard_map/while/body/eval_jaxpr/ppermute | solution.py:25
  111.8 6.1 %collective-permute-done.7 = bf16[256,1024]{1,0:T(8,128)(2,1)S(1)} collective-permute-done((bf16[256,1024]{1,0:T(8,128)(2,1)S(1)}, bf16[256,1024]{1,0:T(8,128)(2,1)S(1)}, u32[]{:S(2)}, u32[]{:S(2)}) %collective-permute-start.7) | collective-permute-done | bytes 524320 | tf_op jit(solution)/shard_map/while/body/eval_jaxpr/ppermute | solution.py:25
  118.7 1.1 broadcast_select_fusion.4
  121.3 1.7 %collective-permute-start.1 = (bf16[1,16,1024]{2,1,0:T(8,128)(2,1)S(1)}, bf16[1,16,1024]{2,1,0:T(8,128)(2,1)S(1)}, u32[]{:S(2)}, u32[]{:S(2)}) collective-permute-start(bf16[1,16,1024]{2,1,0:T(8,128)(2,1)S(1)} %get-tuple-element.460), channel_id=1, source_target_pairs={{0,6},{1,7},{2,0},{3,1},{4,2},{5,3},{6,4},{7,5},{8,14},{9,15},{10,... | collective-permute-start | bytes 98312 | tf_op jit(solution)/shard_map/while/body/eval_jaxpr/ppermute | solution.py:17
  123.3 1.9 %collective-permute-start.3 = (bf16[1,16,1024]{2,1,0:T(8,128)(2,1)S(1)}, bf16[1,16,1024]{2,1,0:T(8,128)(2,1)S(1)}, u32[]{:S(2)}, u32[]{:S(2)}) collective-permute-start(bf16[1,16,1024]{2,1,0:T(8,128)(2,1)S(1)} %get-tuple-element.462), channel_id=1, source_target_pairs={{0,4},{1,5},{2,6},{3,7},{4,0},{5,1},{6,2},{7,3},{8,12},{9,13},{10,... | collective-permute-start | bytes 98312 | tf_op jit(solution)/shard_map/while/body/eval_jaxpr/ppermute | solution.py:17
  125.4 1.2 collective-permute-start.5
  127.7 2.1 %collective-permute-done.4 = bf16[1,16,1024]{2,1,0:T(8,128)(2,1)S(1)} collective-permute-done((bf16[1,16,1024]{2,1,0:T(8,128)(2,1)S(1)}, bf16[1,16,1024]{2,1,0:T(8,128)(2,1)S(1)}, u32[]{:S(2)}, u32[]{:S(2)}) %collective-permute-start.4) | collective-permute-done | bytes 32800 | tf_op jit(solution)/shard_map/while/body/eval_jaxpr/ppermute | solution.py:17
  129.9 2.1 %collective-permute-done.6 = bf16[1,16,1024]{2,1,0:T(8,128)(2,1)S(1)} collective-permute-done((bf16[1,16,1024]{2,1,0:T(8,128)(2,1)S(1)}, bf16[1,16,1024]{2,1,0:T(8,128)(2,1)S(1)}, u32[]{:S(2)}, u32[]{:S(2)}) %collective-permute-start.6) | collective-permute-done | bytes 32800 | tf_op jit(solution)/shard_map/while/body/eval_jaxpr/ppermute | solution.py:17
  132.2 7.2 %collective-permute-start.7 = (bf16[256,1024]{1,0:T(8,128)(2,1)S(1)}, bf16[256,1024]{1,0:T(8,128)(2,1)S(1)}, u32[]{:S(2)}, u32[]{:S(2)}) collective-permute-start(bf16[256,1024]{1,0:T(8,128)(2,1)S(1)} %get-tuple-element.467), channel_id=1, source_target_pairs={{0,8},{8,16},{16,24},{1,9},{9,17},{17,25},{2,10},{10,18},{18,26},{... | collective-permute-start | bytes 1572872 | tf_op jit(solution)/shard_map/while/body/eval_jaxpr/ppermute | solution.py:25
  139.5 6.1 %collective-permute-done.7 = bf16[256,1024]{1,0:T(8,128)(2,1)S(1)} collective-permute-done((bf16[256,1024]{1,0:T(8,128)(2,1)S(1)}, bf16[256,1024]{1,0:T(8,128)(2,1)S(1)}, u32[]{:S(2)}, u32[]{:S(2)}) %collective-permute-start.7) | collective-permute-done | bytes 524320 | tf_op jit(solution)/shard_map/while/body/eval_jaxpr/ppermute | solution.py:25
  (159 shorter events, 20.1 us)
Async XLA Ops:
  2.2 15.7 %copy-start.1 = (s32[2,2,4]{2,1,0:T(2,128)S(1)}, s32[2,2,4]{2,1,0:T(2,128)}, u32[]{:S(2)}) copy-start(s32[2,2,4]{2,1,0:T(2,128)} %get-tuple-element.518) | copy-start | bytes 196 | tf_op jit(solution)/shard_map/while
  3.4 7.7 %collective-permute-start = (bf16[1,16,1024]{2,1,0:T(8,128)(2,1)S(1)}, bf16[1,16,1024]{2,1,0:T(8,128)(2,1)S(1)}, u32[]{:S(2)}, u32[]{:S(2)}) collective-permute-start(bf16[1,16,1024]{2,1,0:T(8,128)(2,1)S(1)} %get-tuple-element.459), channel_id=1, source_target_pairs={{0,7},{1,0},{2,1},{3,2},{4,3},{5,4},{6,5},{7,6},{8,15},{9,8},{10,9... | collective-permute-start | bytes 98312 | tf_op jit(solution)/shard_map/while/body/eval_jaxpr/ppermute | solution.py:17
  8.5 3.9 %collective-permute-start.1 = (bf16[1,16,1024]{2,1,0:T(8,128)(2,1)S(1)}, bf16[1,16,1024]{2,1,0:T(8,128)(2,1)S(1)}, u32[]{:S(2)}, u32[]{:S(2)}) collective-permute-start(bf16[1,16,1024]{2,1,0:T(8,128)(2,1)S(1)} %get-tuple-element.460), channel_id=1, source_target_pairs={{0,6},{1,7},{2,0},{3,1},{4,2},{5,3},{6,4},{7,5},{8,14},{9,15},{10,... | collective-permute-start | bytes 98312 | tf_op jit(solution)/shard_map/while/body/eval_jaxpr/ppermute | solution.py:17
  8.7 4.9 %collective-permute-start.2 = (bf16[1,16,1024]{2,1,0:T(8,128)(2,1)S(1)}, bf16[1,16,1024]{2,1,0:T(8,128)(2,1)S(1)}, u32[]{:S(2)}, u32[]{:S(2)}) collective-permute-start(bf16[1,16,1024]{2,1,0:T(8,128)(2,1)S(1)} %get-tuple-element.461), channel_id=1, source_target_pairs={{0,5},{1,6},{2,7},{3,0},{4,1},{5,2},{6,3},{7,4},{8,13},{9,14},{10,... | collective-permute-start | bytes 98312 | tf_op jit(solution)/shard_map/while/body/eval_jaxpr/ppermute | solution.py:17
  8.7 4.9 %collective-permute-start.3 = (bf16[1,16,1024]{2,1,0:T(8,128)(2,1)S(1)}, bf16[1,16,1024]{2,1,0:T(8,128)(2,1)S(1)}, u32[]{:S(2)}, u32[]{:S(2)}) collective-permute-start(bf16[1,16,1024]{2,1,0:T(8,128)(2,1)S(1)} %get-tuple-element.462), channel_id=1, source_target_pairs={{0,4},{1,5},{2,6},{3,7},{4,0},{5,1},{6,2},{7,3},{8,12},{9,13},{10,... | collective-permute-start | bytes 98312 | tf_op jit(solution)/shard_map/while/body/eval_jaxpr/ppermute | solution.py:17
  11.1 4.7 %collective-permute-start.4 = (bf16[1,16,1024]{2,1,0:T(8,128)(2,1)S(1)}, bf16[1,16,1024]{2,1,0:T(8,128)(2,1)S(1)}, u32[]{:S(2)}, u32[]{:S(2)}) collective-permute-start(bf16[1,16,1024]{2,1,0:T(8,128)(2,1)S(1)} %get-tuple-element.463), channel_id=1, source_target_pairs={{0,3},{1,4},{2,5},{3,6},{4,7},{5,0},{6,1},{7,2},{8,11},{9,12},{10,... | collective-permute-start | bytes 98312 | tf_op jit(solution)/shard_map/while/body/eval_jaxpr/ppermute | solution.py:17
  11.1 5.8 %collective-permute-start.5 = (bf16[1,16,1024]{2,1,0:T(8,128)(2,1)S(1)}, bf16[1,16,1024]{2,1,0:T(8,128)(2,1)S(1)}, u32[]{:S(2)}, u32[]{:S(2)}) collective-permute-start(bf16[1,16,1024]{2,1,0:T(8,128)(2,1)S(1)} %get-tuple-element.464), channel_id=1, source_target_pairs={{0,2},{1,3},{2,4},{3,5},{4,6},{5,7},{6,0},{7,1},{8,10},{9,11},{10,... | collective-permute-start | bytes 98312 | tf_op jit(solution)/shard_map/while/body/eval_jaxpr/ppermute | solution.py:17
  12.4 5.5 %collective-permute-start.6 = (bf16[1,16,1024]{2,1,0:T(8,128)(2,1)S(1)}, bf16[1,16,1024]{2,1,0:T(8,128)(2,1)S(1)}, u32[]{:S(2)}, u32[]{:S(2)}) collective-permute-start(bf16[1,16,1024]{2,1,0:T(8,128)(2,1)S(1)} %get-tuple-element.465), channel_id=1, source_target_pairs={{0,1},{1,2},{2,3},{3,4},{4,5},{5,6},{6,7},{7,0},{8,9},{9,10},{10,1... | collective-permute-start | bytes 98312 | tf_op jit(solution)/shard_map/while/body/eval_jaxpr/ppermute | solution.py:17
  18.0 12.6 %collective-permute-start.7 = (bf16[256,1024]{1,0:T(8,128)(2,1)S(1)}, bf16[256,1024]{1,0:T(8,128)(2,1)S(1)}, u32[]{:S(2)}, u32[]{:S(2)}) collective-permute-start(bf16[256,1024]{1,0:T(8,128)(2,1)S(1)} %get-tuple-element.467), channel_id=1, source_target_pairs={{0,8},{8,16},{16,24},{1,9},{9,17},{17,25},{2,10},{10,18},{18,26},{... | collective-permute-start | bytes 1572872 | tf_op jit(solution)/shard_map/while/body/eval_jaxpr/ppermute | solution.py:25
  32.6 12.9 %copy-start.1 = (s32[2,2,4]{2,1,0:T(2,128)S(1)}, s32[2,2,4]{2,1,0:T(2,128)}, u32[]{:S(2)}) copy-start(s32[2,2,4]{2,1,0:T(2,128)} %get-tuple-element.518) | copy-start | bytes 196 | tf_op jit(solution)/shard_map/while
  33.7 4.5 %collective-permute-start = (bf16[1,16,1024]{2,1,0:T(8,128)(2,1)S(1)}, bf16[1,16,1024]{2,1,0:T(8,128)(2,1)S(1)}, u32[]{:S(2)}, u32[]{:S(2)}) collective-permute-start(bf16[1,16,1024]{2,1,0:T(8,128)(2,1)S(1)} %get-tuple-element.459), channel_id=1, source_target_pairs={{0,7},{1,0},{2,1},{3,2},{4,3},{5,4},{6,5},{7,6},{8,15},{9,8},{10,9... | collective-permute-start | bytes 98312 | tf_op jit(solution)/shard_map/while/body/eval_jaxpr/ppermute | solution.py:17
  33.7 6.2 %collective-permute-start.1 = (bf16[1,16,1024]{2,1,0:T(8,128)(2,1)S(1)}, bf16[1,16,1024]{2,1,0:T(8,128)(2,1)S(1)}, u32[]{:S(2)}, u32[]{:S(2)}) collective-permute-start(bf16[1,16,1024]{2,1,0:T(8,128)(2,1)S(1)} %get-tuple-element.460), channel_id=1, source_target_pairs={{0,6},{1,7},{2,0},{3,1},{4,2},{5,3},{6,4},{7,5},{8,14},{9,15},{10,... | collective-permute-start | bytes 98312 | tf_op jit(solution)/shard_map/while/body/eval_jaxpr/ppermute | solution.py:17
  34.9 6.5 %collective-permute-start.2 = (bf16[1,16,1024]{2,1,0:T(8,128)(2,1)S(1)}, bf16[1,16,1024]{2,1,0:T(8,128)(2,1)S(1)}, u32[]{:S(2)}, u32[]{:S(2)}) collective-permute-start(bf16[1,16,1024]{2,1,0:T(8,128)(2,1)S(1)} %get-tuple-element.461), channel_id=1, source_target_pairs={{0,5},{1,6},{2,7},{3,0},{4,1},{5,2},{6,3},{7,4},{8,13},{9,14},{10,... | collective-permute-start | bytes 98312 | tf_op jit(solution)/shard_map/while/body/eval_jaxpr/ppermute | solution.py:17
  36.3 5.2 %collective-permute-start.3 = (bf16[1,16,1024]{2,1,0:T(8,128)(2,1)S(1)}, bf16[1,16,1024]{2,1,0:T(8,128)(2,1)S(1)}, u32[]{:S(2)}, u32[]{:S(2)}) collective-permute-start(bf16[1,16,1024]{2,1,0:T(8,128)(2,1)S(1)} %get-tuple-element.462), channel_id=1, source_target_pairs={{0,4},{1,5},{2,6},{3,7},{4,0},{5,1},{6,2},{7,3},{8,12},{9,13},{10,... | collective-permute-start | bytes 98312 | tf_op jit(solution)/shard_map/while/body/eval_jaxpr/ppermute | solution.py:17
  38.2 4.6 %collective-permute-start.4 = (bf16[1,16,1024]{2,1,0:T(8,128)(2,1)S(1)}, bf16[1,16,1024]{2,1,0:T(8,128)(2,1)S(1)}, u32[]{:S(2)}, u32[]{:S(2)}) collective-permute-start(bf16[1,16,1024]{2,1,0:T(8,128)(2,1)S(1)} %get-tuple-element.463), channel_id=1, source_target_pairs={{0,3},{1,4},{2,5},{3,6},{4,7},{5,0},{6,1},{7,2},{8,11},{9,12},{10,... | collective-permute-start | bytes 98312 | tf_op jit(solution)/shard_map/while/body/eval_jaxpr/ppermute | solution.py:17
  38.2 4.6 %collective-permute-start.5 = (bf16[1,16,1024]{2,1,0:T(8,128)(2,1)S(1)}, bf16[1,16,1024]{2,1,0:T(8,128)(2,1)S(1)}, u32[]{:S(2)}, u32[]{:S(2)}) collective-permute-start(bf16[1,16,1024]{2,1,0:T(8,128)(2,1)S(1)} %get-tuple-element.464), channel_id=1, source_target_pairs={{0,2},{1,3},{2,4},{3,5},{4,6},{5,7},{6,0},{7,1},{8,10},{9,11},{10,... | collective-permute-start | bytes 98312 | tf_op jit(solution)/shard_map/while/body/eval_jaxpr/ppermute | solution.py:17
  40.0 5.5 %collective-permute-start.6 = (bf16[1,16,1024]{2,1,0:T(8,128)(2,1)S(1)}, bf16[1,16,1024]{2,1,0:T(8,128)(2,1)S(1)}, u32[]{:S(2)}, u32[]{:S(2)}) collective-permute-start(bf16[1,16,1024]{2,1,0:T(8,128)(2,1)S(1)} %get-tuple-element.465), channel_id=1, source_target_pairs={{0,1},{1,2},{2,3},{3,4},{4,5},{5,6},{6,7},{7,0},{8,9},{9,10},{10,1... | collective-permute-start | bytes 98312 | tf_op jit(solution)/shard_map/while/body/eval_jaxpr/ppermute | solution.py:17
  45.6 1.8 %copy-start.2 = (bf16[1024,1024]{1,0:T(8,128)(2,1)S(1)}, bf16[1024,1024]{1,0:T(8,128)(2,1)}, u32[]{:S(2)}) copy-start(bf16[1024,1024]{1,0:T(8,128)(2,1)} %get-tuple-element.319) | copy-start | bytes 6291460 | tf_op jit(solution)/shard_map/while/body/eval_jaxpr/cond
  48.1 10.5 %collective-permute-start.7 = (bf16[256,1024]{1,0:T(8,128)(2,1)S(1)}, bf16[256,1024]{1,0:T(8,128)(2,1)S(1)}, u32[]{:S(2)}, u32[]{:S(2)}) collective-permute-start(bf16[256,1024]{1,0:T(8,128)(2,1)S(1)} %get-tuple-element.467), channel_id=1, source_target_pairs={{0,8},{8,16},{16,24},{1,9},{9,17},{17,25},{2,10},{10,18},{18,26},{... | collective-permute-start | bytes 1572872 | tf_op jit(solution)/shard_map/while/body/eval_jaxpr/ppermute | solution.py:25
  60.5 12.0 %copy-start.1 = (s32[2,2,4]{2,1,0:T(2,128)S(1)}, s32[2,2,4]{2,1,0:T(2,128)}, u32[]{:S(2)}) copy-start(s32[2,2,4]{2,1,0:T(2,128)} %get-tuple-element.518) | copy-start | bytes 196 | tf_op jit(solution)/shard_map/while
  61.7 3.8 %collective-permute-start = (bf16[1,16,1024]{2,1,0:T(8,128)(2,1)S(1)}, bf16[1,16,1024]{2,1,0:T(8,128)(2,1)S(1)}, u32[]{:S(2)}, u32[]{:S(2)}) collective-permute-start(bf16[1,16,1024]{2,1,0:T(8,128)(2,1)S(1)} %get-tuple-element.459), channel_id=1, source_target_pairs={{0,7},{1,0},{2,1},{3,2},{4,3},{5,4},{6,5},{7,6},{8,15},{9,8},{10,9... | collective-permute-start | bytes 98312 | tf_op jit(solution)/shard_map/while/body/eval_jaxpr/ppermute | solution.py:17
  61.9 5.1 %collective-permute-start.1 = (bf16[1,16,1024]{2,1,0:T(8,128)(2,1)S(1)}, bf16[1,16,1024]{2,1,0:T(8,128)(2,1)S(1)}, u32[]{:S(2)}, u32[]{:S(2)}) collective-permute-start(bf16[1,16,1024]{2,1,0:T(8,128)(2,1)S(1)} %get-tuple-element.460), channel_id=1, source_target_pairs={{0,6},{1,7},{2,0},{3,1},{4,2},{5,3},{6,4},{7,5},{8,14},{9,15},{10,... | collective-permute-start | bytes 98312 | tf_op jit(solution)/shard_map/while/body/eval_jaxpr/ppermute | solution.py:17
  62.5 5.4 %collective-permute-start.2 = (bf16[1,16,1024]{2,1,0:T(8,128)(2,1)S(1)}, bf16[1,16,1024]{2,1,0:T(8,128)(2,1)S(1)}, u32[]{:S(2)}, u32[]{:S(2)}) collective-permute-start(bf16[1,16,1024]{2,1,0:T(8,128)(2,1)S(1)} %get-tuple-element.461), channel_id=1, source_target_pairs={{0,5},{1,6},{2,7},{3,0},{4,1},{5,2},{6,3},{7,4},{8,13},{9,14},{10,... | collective-permute-start | bytes 98312 | tf_op jit(solution)/shard_map/while/body/eval_jaxpr/ppermute | solution.py:17
  62.8 5.1 %collective-permute-start.3 = (bf16[1,16,1024]{2,1,0:T(8,128)(2,1)S(1)}, bf16[1,16,1024]{2,1,0:T(8,128)(2,1)S(1)}, u32[]{:S(2)}, u32[]{:S(2)}) collective-permute-start(bf16[1,16,1024]{2,1,0:T(8,128)(2,1)S(1)} %get-tuple-element.462), channel_id=1, source_target_pairs={{0,4},{1,5},{2,6},{3,7},{4,0},{5,1},{6,2},{7,3},{8,12},{9,13},{10,... | collective-permute-start | bytes 98312 | tf_op jit(solution)/shard_map/while/body/eval_jaxpr/ppermute | solution.py:17
  65.3 4.6 %collective-permute-start.4 = (bf16[1,16,1024]{2,1,0:T(8,128)(2,1)S(1)}, bf16[1,16,1024]{2,1,0:T(8,128)(2,1)S(1)}, u32[]{:S(2)}, u32[]{:S(2)}) collective-permute-start(bf16[1,16,1024]{2,1,0:T(8,128)(2,1)S(1)} %get-tuple-element.463), channel_id=1, source_target_pairs={{0,3},{1,4},{2,5},{3,6},{4,7},{5,0},{6,1},{7,2},{8,11},{9,12},{10,... | collective-permute-start | bytes 98312 | tf_op jit(solution)/shard_map/while/body/eval_jaxpr/ppermute | solution.py:17
  65.4 5.0 %collective-permute-start.5 = (bf16[1,16,1024]{2,1,0:T(8,128)(2,1)S(1)}, bf16[1,16,1024]{2,1,0:T(8,128)(2,1)S(1)}, u32[]{:S(2)}, u32[]{:S(2)}) collective-permute-start(bf16[1,16,1024]{2,1,0:T(8,128)(2,1)S(1)} %get-tuple-element.464), channel_id=1, source_target_pairs={{0,2},{1,3},{2,4},{3,5},{4,6},{5,7},{6,0},{7,1},{8,10},{9,11},{10,... | collective-permute-start | bytes 98312 | tf_op jit(solution)/shard_map/while/body/eval_jaxpr/ppermute | solution.py:17
  67.0 5.5 %collective-permute-start.6 = (bf16[1,16,1024]{2,1,0:T(8,128)(2,1)S(1)}, bf16[1,16,1024]{2,1,0:T(8,128)(2,1)S(1)}, u32[]{:S(2)}, u32[]{:S(2)}) collective-permute-start(bf16[1,16,1024]{2,1,0:T(8,128)(2,1)S(1)} %get-tuple-element.465), channel_id=1, source_target_pairs={{0,1},{1,2},{2,3},{3,4},{4,5},{5,6},{6,7},{7,0},{8,9},{9,10},{10,1... | collective-permute-start | bytes 98312 | tf_op jit(solution)/shard_map/while/body/eval_jaxpr/ppermute | solution.py:17
  72.6 1.8 %copy-start.2 = (bf16[1024,1024]{1,0:T(8,128)(2,1)S(1)}, bf16[1024,1024]{1,0:T(8,128)(2,1)}, u32[]{:S(2)}) copy-start(bf16[1024,1024]{1,0:T(8,128)(2,1)} %get-tuple-element.319) | copy-start | bytes 6291460 | tf_op jit(solution)/shard_map/while/body/eval_jaxpr/cond
  75.2 13.3 %collective-permute-start.7 = (bf16[256,1024]{1,0:T(8,128)(2,1)S(1)}, bf16[256,1024]{1,0:T(8,128)(2,1)S(1)}, u32[]{:S(2)}, u32[]{:S(2)}) collective-permute-start(bf16[256,1024]{1,0:T(8,128)(2,1)S(1)} %get-tuple-element.467), channel_id=1, source_target_pairs={{0,8},{8,16},{16,24},{1,9},{9,17},{17,25},{2,10},{10,18},{18,26},{... | collective-permute-start | bytes 1572872 | tf_op jit(solution)/shard_map/while/body/eval_jaxpr/ppermute | solution.py:25
  90.4 11.7 %copy-start.1 = (s32[2,2,4]{2,1,0:T(2,128)S(1)}, s32[2,2,4]{2,1,0:T(2,128)}, u32[]{:S(2)}) copy-start(s32[2,2,4]{2,1,0:T(2,128)} %get-tuple-element.518) | copy-start | bytes 196 | tf_op jit(solution)/shard_map/while
  91.6 3.9 %collective-permute-start = (bf16[1,16,1024]{2,1,0:T(8,128)(2,1)S(1)}, bf16[1,16,1024]{2,1,0:T(8,128)(2,1)S(1)}, u32[]{:S(2)}, u32[]{:S(2)}) collective-permute-start(bf16[1,16,1024]{2,1,0:T(8,128)(2,1)S(1)} %get-tuple-element.459), channel_id=1, source_target_pairs={{0,7},{1,0},{2,1},{3,2},{4,3},{5,4},{6,5},{7,6},{8,15},{9,8},{10,9... | collective-permute-start | bytes 98312 | tf_op jit(solution)/shard_map/while/body/eval_jaxpr/ppermute | solution.py:17
  91.6 5.0 %collective-permute-start.1 = (bf16[1,16,1024]{2,1,0:T(8,128)(2,1)S(1)}, bf16[1,16,1024]{2,1,0:T(8,128)(2,1)S(1)}, u32[]{:S(2)}, u32[]{:S(2)}) collective-permute-start(bf16[1,16,1024]{2,1,0:T(8,128)(2,1)S(1)} %get-tuple-element.460), channel_id=1, source_target_pairs={{0,6},{1,7},{2,0},{3,1},{4,2},{5,3},{6,4},{7,5},{8,14},{9,15},{10,... | collective-permute-start | bytes 98312 | tf_op jit(solution)/shard_map/while/body/eval_jaxpr/ppermute | solution.py:17
  93.1 5.0 %collective-permute-start.2 = (bf16[1,16,1024]{2,1,0:T(8,128)(2,1)S(1)}, bf16[1,16,1024]{2,1,0:T(8,128)(2,1)S(1)}, u32[]{:S(2)}, u32[]{:S(2)}) collective-permute-start(bf16[1,16,1024]{2,1,0:T(8,128)(2,1)S(1)} %get-tuple-element.461), channel_id=1, source_target_pairs={{0,5},{1,6},{2,7},{3,0},{4,1},{5,2},{6,3},{7,4},{8,13},{9,14},{10,... | collective-permute-start | bytes 98312 | tf_op jit(solution)/shard_map/while/body/eval_jaxpr/ppermute | solution.py:17
  93.1 5.0 %collective-permute-start.3 = (bf16[1,16,1024]{2,1,0:T(8,128)(2,1)S(1)}, bf16[1,16,1024]{2,1,0:T(8,128)(2,1)S(1)}, u32[]{:S(2)}, u32[]{:S(2)}) collective-permute-start(bf16[1,16,1024]{2,1,0:T(8,128)(2,1)S(1)} %get-tuple-element.462), channel_id=1, source_target_pairs={{0,4},{1,5},{2,6},{3,7},{4,0},{5,1},{6,2},{7,3},{8,12},{9,13},{10,... | collective-permute-start | bytes 98312 | tf_op jit(solution)/shard_map/while/body/eval_jaxpr/ppermute | solution.py:17
  95.2 4.6 %collective-permute-start.4 = (bf16[1,16,1024]{2,1,0:T(8,128)(2,1)S(1)}, bf16[1,16,1024]{2,1,0:T(8,128)(2,1)S(1)}, u32[]{:S(2)}, u32[]{:S(2)}) collective-permute-start(bf16[1,16,1024]{2,1,0:T(8,128)(2,1)S(1)} %get-tuple-element.463), channel_id=1, source_target_pairs={{0,3},{1,4},{2,5},{3,6},{4,7},{5,0},{6,1},{7,2},{8,11},{9,12},{10,... | collective-permute-start | bytes 98312 | tf_op jit(solution)/shard_map/while/body/eval_jaxpr/ppermute | solution.py:17
  95.5 4.7 %collective-permute-start.5 = (bf16[1,16,1024]{2,1,0:T(8,128)(2,1)S(1)}, bf16[1,16,1024]{2,1,0:T(8,128)(2,1)S(1)}, u32[]{:S(2)}, u32[]{:S(2)}) collective-permute-start(bf16[1,16,1024]{2,1,0:T(8,128)(2,1)S(1)} %get-tuple-element.464), channel_id=1, source_target_pairs={{0,2},{1,3},{2,4},{3,5},{4,6},{5,7},{6,0},{7,1},{8,10},{9,11},{10,... | collective-permute-start | bytes 98312 | tf_op jit(solution)/shard_map/while/body/eval_jaxpr/ppermute | solution.py:17
  96.7 5.5 %collective-permute-start.6 = (bf16[1,16,1024]{2,1,0:T(8,128)(2,1)S(1)}, bf16[1,16,1024]{2,1,0:T(8,128)(2,1)S(1)}, u32[]{:S(2)}, u32[]{:S(2)}) collective-permute-start(bf16[1,16,1024]{2,1,0:T(8,128)(2,1)S(1)} %get-tuple-element.465), channel_id=1, source_target_pairs={{0,1},{1,2},{2,3},{3,4},{4,5},{5,6},{6,7},{7,0},{8,9},{9,10},{10,1... | collective-permute-start | bytes 98312 | tf_op jit(solution)/shard_map/while/body/eval_jaxpr/ppermute | solution.py:17
  102.3 15.6 %collective-permute-start.7 = (bf16[256,1024]{1,0:T(8,128)(2,1)S(1)}, bf16[256,1024]{1,0:T(8,128)(2,1)S(1)}, u32[]{:S(2)}, u32[]{:S(2)}) collective-permute-start(bf16[256,1024]{1,0:T(8,128)(2,1)S(1)} %get-tuple-element.467), channel_id=1, source_target_pairs={{0,8},{8,16},{16,24},{1,9},{9,17},{17,25},{2,10},{10,18},{18,26},{... | collective-permute-start | bytes 1572872 | tf_op jit(solution)/shard_map/while/body/eval_jaxpr/ppermute | solution.py:25
  119.8 12.3 %copy-start.1 = (s32[2,2,4]{2,1,0:T(2,128)S(1)}, s32[2,2,4]{2,1,0:T(2,128)}, u32[]{:S(2)}) copy-start(s32[2,2,4]{2,1,0:T(2,128)} %get-tuple-element.518) | copy-start | bytes 196 | tf_op jit(solution)/shard_map/while
  120.9 4.5 %collective-permute-start = (bf16[1,16,1024]{2,1,0:T(8,128)(2,1)S(1)}, bf16[1,16,1024]{2,1,0:T(8,128)(2,1)S(1)}, u32[]{:S(2)}, u32[]{:S(2)}) collective-permute-start(bf16[1,16,1024]{2,1,0:T(8,128)(2,1)S(1)} %get-tuple-element.459), channel_id=1, source_target_pairs={{0,7},{1,0},{2,1},{3,2},{4,3},{5,4},{6,5},{7,6},{8,15},{9,8},{10,9... | collective-permute-start | bytes 98312 | tf_op jit(solution)/shard_map/while/body/eval_jaxpr/ppermute | solution.py:17
  121.3 5.3 %collective-permute-start.1 = (bf16[1,16,1024]{2,1,0:T(8,128)(2,1)S(1)}, bf16[1,16,1024]{2,1,0:T(8,128)(2,1)S(1)}, u32[]{:S(2)}, u32[]{:S(2)}) collective-permute-start(bf16[1,16,1024]{2,1,0:T(8,128)(2,1)S(1)} %get-tuple-element.460), channel_id=1, source_target_pairs={{0,6},{1,7},{2,0},{3,1},{4,2},{5,3},{6,4},{7,5},{8,14},{9,15},{10,... | collective-permute-start | bytes 98312 | tf_op jit(solution)/shard_map/while/body/eval_jaxpr/ppermute | solution.py:17
  123.0 4.5 %collective-permute-start.2 = (bf16[1,16,1024]{2,1,0:T(8,128)(2,1)S(1)}, bf16[1,16,1024]{2,1,0:T(8,128)(2,1)S(1)}, u32[]{:S(2)}, u32[]{:S(2)}) collective-permute-start(bf16[1,16,1024]{2,1,0:T(8,128)(2,1)S(1)} %get-tuple-element.461), channel_id=1, source_target_pairs={{0,5},{1,6},{2,7},{3,0},{4,1},{5,2},{6,3},{7,4},{8,13},{9,14},{10,... | collective-permute-start | bytes 98312 | tf_op jit(solution)/shard_map/while/body/eval_jaxpr/ppermute | solution.py:17
  123.3 4.4 %collective-permute-start.3 = (bf16[1,16,1024]{2,1,0:T(8,128)(2,1)S(1)}, bf16[1,16,1024]{2,1,0:T(8,128)(2,1)S(1)}, u32[]{:S(2)}, u32[]{:S(2)}) collective-permute-start(bf16[1,16,1024]{2,1,0:T(8,128)(2,1)S(1)} %get-tuple-element.462), channel_id=1, source_target_pairs={{0,4},{1,5},{2,6},{3,7},{4,0},{5,1},{6,2},{7,3},{8,12},{9,13},{10,... | collective-permute-start | bytes 98312 | tf_op jit(solution)/shard_map/while/body/eval_jaxpr/ppermute | solution.py:17
  125.2 4.6 %collective-permute-start.4 = (bf16[1,16,1024]{2,1,0:T(8,128)(2,1)S(1)}, bf16[1,16,1024]{2,1,0:T(8,128)(2,1)S(1)}, u32[]{:S(2)}, u32[]{:S(2)}) collective-permute-start(bf16[1,16,1024]{2,1,0:T(8,128)(2,1)S(1)} %get-tuple-element.463), channel_id=1, source_target_pairs={{0,3},{1,4},{2,5},{3,6},{4,7},{5,0},{6,1},{7,2},{8,11},{9,12},{10,... | collective-permute-start | bytes 98312 | tf_op jit(solution)/shard_map/while/body/eval_jaxpr/ppermute | solution.py:17
  125.4 4.6 %collective-permute-start.5 = (bf16[1,16,1024]{2,1,0:T(8,128)(2,1)S(1)}, bf16[1,16,1024]{2,1,0:T(8,128)(2,1)S(1)}, u32[]{:S(2)}, u32[]{:S(2)}) collective-permute-start(bf16[1,16,1024]{2,1,0:T(8,128)(2,1)S(1)} %get-tuple-element.464), channel_id=1, source_target_pairs={{0,2},{1,3},{2,4},{3,5},{4,6},{5,7},{6,0},{7,1},{8,10},{9,11},{10,... | collective-permute-start | bytes 98312 | tf_op jit(solution)/shard_map/while/body/eval_jaxpr/ppermute | solution.py:17
  126.6 5.5 %collective-permute-start.6 = (bf16[1,16,1024]{2,1,0:T(8,128)(2,1)S(1)}, bf16[1,16,1024]{2,1,0:T(8,128)(2,1)S(1)}, u32[]{:S(2)}, u32[]{:S(2)}) collective-permute-start(bf16[1,16,1024]{2,1,0:T(8,128)(2,1)S(1)} %get-tuple-element.465), channel_id=1, source_target_pairs={{0,1},{1,2},{2,3},{3,4},{4,5},{5,6},{6,7},{7,0},{8,9},{9,10},{10,1... | collective-permute-start | bytes 98312 | tf_op jit(solution)/shard_map/while/body/eval_jaxpr/ppermute | solution.py:17
  132.2 13.3 %collective-permute-start.7 = (bf16[256,1024]{1,0:T(8,128)(2,1)S(1)}, bf16[256,1024]{1,0:T(8,128)(2,1)S(1)}, u32[]{:S(2)}, u32[]{:S(2)}) collective-permute-start(bf16[256,1024]{1,0:T(8,128)(2,1)S(1)} %get-tuple-element.467), channel_id=1, source_target_pairs={{0,8},{8,16},{16,24},{1,9},{9,17},{17,25},{2,10},{10,18},{18,26},{... | collective-permute-start | bytes 1572872 | tf_op jit(solution)/shard_map/while/body/eval_jaxpr/ppermute | solution.py:25
  145.6 1.0 copy-start
